TPU v7x, 32 devices: a whole 2x2x4 slice. The times are simulated.
32 devices in a mesh: cells: 16 (over z, y, x), feat: 2 (over core).
Axes of the slice: x: 2, y: 2, z: 4, core: 2. Of those that a mesh axis runs over, the one named last changes fastest.
Arguments:
- features: float32 [32768, 4096], P('cells', 'feat'), may hold values from -6 to 6
- labels: int32 [32768], P('cells'), may hold values from 0 to 7
- weights: float32 [8, 4096], P(None, 'feat'), may hold values from -0.09375 to 0.09375
Outputs:
- new_weights: float32 [8, 4096], P(None, 'feat')
- new_logits: float32 [8, 32768], P(None, 'cells')
All inputs are finite; a program needn't handle non-finite values.
Results may differ from a plain program's by a relative error of at most 0.00018.
Values sent between devices are 32-bit elements; how exact they have to be, the bound alone decides.
A program may use at most 64 MiB of HBM per device.

v0:
```python
import jax
import jax.numpy as jnp
from jax import lax
from jax.sharding import PartitionSpec as P

ITERS = 2


HIGH = lax.Precision.HIGHEST
RIDGE = 0.01


def on_device(features, labels, weights):
    rows = features.shape[0]
    classes = weights.shape[0]
    count = rows * lax.axis_size("cells") * 1.0

    def row_sums(coeffs):
        local_rows = lax.dot_general(
            coeffs,
            features,
            (((1,), (1,)), ((), ())),
            precision=HIGH,
            preferred_element_type=jnp.float32,
        )
        summed = lax.psum(local_rows, "feat")
        return (summed, summed[classes:])

    def collect(terms):
        return lax.psum(jnp.dot(terms, features, precision=HIGH), "cells")

    def total(packed):
        return lax.psum(packed, "feat")

    def inner(left, right):
        return total(jnp.sum(left * right))

    logits, unused = row_sums(weights)
    expo = jnp.exp(logits)
    probs = expo / jnp.sum(expo, axis=0, keepdims=True)
    onehot = (labels[None, :] == jnp.arange(classes, dtype=jnp.int32)[:, None]).astype(jnp.float32)
    grad = collect(probs - onehot) / count + RIDGE * weights
    resid = -grad
    direction = resid
    rr_now = jnp.float32(0.0)
    rr_now = inner(resid, resid)
    step = jnp.zeros_like(weights)
    moved = jnp.zeros_like(logits)
    for it in range(ITERS):
        full_direction = direction
        image, unused = row_sums(full_direction)
        curv = probs * image - probs * jnp.sum(probs * image, axis=0, keepdims=True)
        product = collect(curv) / count + RIDGE * direction
        alpha = rr_now / inner(direction, product)
        step = step + alpha * direction
        moved = moved + alpha * image
        resid = resid - alpha * product
        if it + 1 < ITERS:
            rr_next = inner(resid, resid)
            direction = resid + rr_next / rr_now * direction
            rr_now = rr_next
    return (weights + step, logits + moved)


def solution(mesh):
    return jax.shard_map(
        on_device,
        mesh=mesh,
        in_specs=(P("cells", "feat"), P("cells"), P(None, "feat")),
        out_specs=(P(None, "feat"), P(None, "cells")),
        check_vma=False,
    )
```

profile of v0, /device:TPU:0, one launch (start us, length us, event | category | flops | bytes accessed | tf_op | source)
XLA Modules:
  0.0 500.8 jit_solution(12203118077418781199)
XLA Ops:
  7.2 0.0 all-reduce.8.cloned.1.call-start
  7.2 19.7 %fusion.21 = f32[8,2048]{1,0:T(8,128)} fusion(f32[8,2048]{1,0:T(8,128)} %param.5, f32[2048,2048]{1,0:T(8,128)} %param.3), kind=kOutput, calls=%fused_computation.32 | convolution fusion | flops 402653184 | bytes 16908288 | tf_op jit(solution)/shard_map/dot_general | solution.py:19
  26.9 0.0 all-reduce.8.cloned.1.call-update
  27.0 0.0 all-reduce.10.cloned.1.call-start
  27.0 20.5 %all-reduce.8.cloned.1.call-done = f32[8,2048]{1,0:T(8,128)} async-done(((f32[8,2048]{1,0:T(8,128)}), f32[8,2048]{1,0:T(8,128)}) %all-reduce.8.cloned.1.call-update) | async-done | bytes 65552 | tf_op jit(solution)/shard_map/psum | solution.py:26
  47.6 0.9 exponential_reduce_fusion
  48.5 14.2 %fusion.6 = f32[8,2048]{1,0:T(8,128)} fusion(f32[2048,2048]{1,0:T(8,128)} %param.3, s32[2048]{0:T(1024)S(1)} %copy-done.5, f32[8,2048]{1,0:T(8,128)} %all-reduce.8.cloned.1.call-done, f32[2048]{0:T(1024)S(1)} %exponential_reduce_fusion), kind=kOutput, calls=%fused_computation.16 | convolution fusion | flops 402718720 | bytes 16924672 | tf_op jit(solution)/shard_map/dot_general | solution.py:30
  62.6 0.0 all-reduce.10.cloned.1.call-update
  62.6 0.2 all-reduce.12.cloned.1.call-start
  62.9 104.6 %all-reduce.10.cloned.1.call-done = f32[8,2048]{1,0:T(8,128)} async-done(((f32[8,2048]{1,0:T(8,128)}), f32[8,2048]{1,0:T(8,128)}) %all-reduce.10.cloned.1.call-update) | async-done | bytes 65552 | tf_op jit(solution)/shard_map/psum | solution.py:30
  167.5 0.9 multiply_add_fusion.2
  168.3 17.7 %fusion.9 = f32[8,2048]{1,0:T(8,128)} fusion(f32[2048,2048]{1,0:T(8,128)} %param.3, f32[8,2048]{1,0:T(8,128)S(1)} %multiply_add_fusion.2), kind=kOutput, calls=%fused_computation.22 | convolution fusion | flops 402669568 | bytes 16908288 | tf_op jit(solution)/shard_map/dot_general | solution.py:19
  186.0 0.0 all-reduce.12.cloned.1.call-update
  186.0 0.0 all-reduce.14.cloned.1.call-start
  186.1 16.9 %all-reduce.12.cloned.1.call-done = f32[8,2048]{1,0:T(8,128)} async-done(((f32[8,2048]{1,0:T(8,128)}), f32[8,2048]{1,0:T(8,128)}) %all-reduce.12.cloned.1.call-update) | async-done | bytes 65552 | tf_op jit(solution)/shard_map/psum | solution.py:26
  202.9 0.9 fusion.18
  203.8 12.1 %fusion.3 = f32[8,2048]{1,0:T(8,128)} fusion(f32[2048,2048]{1,0:T(8,128)} %param.3, f32[2048]{0:T(1024)S(1)} %fusion.18, f32[8,2048]{1,0:T(8,128)S(1)} %copy-done, f32[2048]{0:T(1024)S(1)} %exponential_reduce_fusion, f32[8,2048]{1,0:T(8,128)} %all-reduce.12.cloned.1.call-done), kind=kOutput, calls=%fused_computation.11 | convolution fusion | flops 402718720 | bytes 16990208 | tf_op jit(solution)/shard_map/dot_general | solution.py:30
  215.9 0.0 all-reduce.16.cloned.1.call-start
  216.0 104.8 %all-reduce.14.cloned.1.call-done = f32[8,2048]{1,0:T(8,128)} async-done(((f32[8,2048]{1,0:T(8,128)}), f32[8,2048]{1,0:T(8,128)}) %all-reduce.14.cloned.1.call-update) | async-done | bytes 65552 | tf_op jit(solution)/shard_map/psum | solution.py:30
  320.8 1.5 multiply_reduce_fusion.2
  322.2 3.1 all-reduce
  326.6 1.5 multiply_reduce_fusion.1
  328.1 3.4 psum.76
  332.8 19.8 %fusion.14 = f32[8,2048]{1,0:T(8,128)} fusion(f32[2048,2048]{1,0:T(8,128)} %param.3, f32[8,2048]{1,0:T(8,128)S(1)} %multiply_add_fusion.2, f32[8,2048]{1,0:T(8,128)} %all-reduce.14.cloned.1.call-done, f32[]{:T(128)S(6)} %div.31, f32[]{:T(128)S(6)} %div.30), kind=kOutput, calls=%fused_computation.27 | convolution fusion | flops 402784256 | bytes 16973832 | tf_op jit(solution)/shard_map/dot_general | solution.py:19
  352.6 0.0 all-reduce.18.cloned.1.call-start
  352.6 16.9 %all-reduce.16.cloned.1.call-done = f32[8,2048]{1,0:T(8,128)} async-done(((f32[8,2048]{1,0:T(8,128)}), f32[8,2048]{1,0:T(8,128)}) %all-reduce.16.cloned.1.call-update) | async-done | bytes 65552 | tf_op jit(solution)/shard_map/psum | solution.py:26
  369.5 0.9 fusion.20
  370.5 12.1 %fusion = f32[8,2048]{1,0:T(8,128)} fusion(f32[2048,2048]{1,0:T(8,128)} %param.3, f32[2048]{0:T(1024)S(1)} %fusion.20, f32[8,2048]{1,0:T(8,128)S(1)} %copy-done, f32[2048]{0:T(1024)S(1)} %exponential_reduce_fusion, f32[8,2048]{1,0:T(8,128)} %all-reduce.16.cloned.1.call-done), kind=kOutput, calls=%fused_computation.3 | convolution fusion | flops 402718720 | bytes 16990208 | tf_op jit(solution)/shard_map/dot_general | solution.py:30
  382.6 104.8 %all-reduce.18.cloned.1.call-done = f32[8,2048]{1,0:T(8,128)} async-done(((f32[8,2048]{1,0:T(8,128)}), f32[8,2048]{1,0:T(8,128)}) %all-reduce.18.cloned.1.call-update) | async-done | bytes 65552 | tf_op jit(solution)/shard_map/psum | solution.py:30
  487.4 1.5 multiply_reduce_fusion
  488.9 3.1 psum.79
  493.3 0.7 add_add_fusion
  (15 shorter events, 0.1 us)
Async XLA Ops:
  7.2 160.3 %copy-start.2 = (f32[8,2048]{1,0:T(8,128)S(1)}, f32[8,2048]{1,0:T(8,128)}, u32[]{:S(2)}) copy-start(f32[8,2048]{1,0:T(8,128)} %param.5) | copy-start | bytes 196612
  7.2 41.3 %copy-start.5 = (s32[2048]{0:T(1024)S(1)}, s32[2048]{0:T(1024)}, u32[]{:S(2)}) copy-start(s32[2048]{0:T(1024)} %param.4) | copy-start | bytes 24580
  7.2 40.4 %all-reduce.8.cloned.1.call-start = ((), (), s32[]{:S(2)}) async-start(), calls=%async_computation | async-start | bytes 131072 | tf_op jit(solution)/shard_map/psum | solution.py:26
  27.0 140.5 %all-reduce.10.cloned.1.call-start = ((), (), s32[]{:S(2)}) async-start(), calls=%async_computation.1 | async-start | bytes 131072 | tf_op jit(solution)/shard_map/psum | solution.py:30
  48.4 154.5 %copy-start = (f32[8,2048]{1,0:T(8,128)S(1)}, f32[8,2048]{1,0:T(8,128)}, u32[]{:S(2)}) copy-start(f32[8,2048]{1,0:T(8,128)} %all-reduce.8.cloned.1.call-done) | copy-start | bytes 196612
  62.6 140.3 %all-reduce.12.cloned.1.call-start = ((), (), s32[]{:S(2)}) async-start(), calls=%async_computation.2 | async-start | bytes 131072 | tf_op jit(solution)/shard_map/psum | solution.py:26
  186.0 134.7 %all-reduce.14.cloned.1.call-start = ((), (), s32[]{:S(2)}) async-start(), calls=%async_computation.3 | async-start | bytes 131072 | tf_op jit(solution)/shard_map/psum | solution.py:30
  215.9 153.6 %all-reduce.16.cloned.1.call-start = ((), (), s32[]{:S(2)}) async-start(), calls=%async_computation.4 | async-start | bytes 131072 | tf_op jit(solution)/shard_map/psum | solution.py:26
  332.8 154.6 %copy-start.1 = (f32[8,2048]{1,0:T(8,128)S(1)}, f32[8,2048]{1,0:T(8,128)}, u32[]{:S(2)}) copy-start(f32[8,2048]{1,0:T(8,128)} %all-reduce.14.cloned.1.call-done) | copy-start | bytes 196612
  332.8 160.5 %copy-start.3 = (f32[8,2048]{1,0:T(8,128)S(1)}, f32[8,2048]{1,0:T(8,128)}, u32[]{:S(2)}) copy-start(f32[8,2048]{1,0:T(8,128)} %all-reduce.12.cloned.1.call-done) | copy-start | bytes 196612
  352.6 134.8 %all-reduce.18.cloned.1.call-start = ((), (), s32[]{:S(2)}) async-start(), calls=%async_computation.5 | async-start | bytes 131072 | tf_op jit(solution)/shard_map/psum | solution.py:30
  369.5 123.8 %copy-start.4 = (f32[8,2048]{1,0:T(8,128)S(1)}, f32[8,2048]{1,0:T(8,128)}, u32[]{:S(2)}) copy-start(f32[8,2048]{1,0:T(8,128)} %all-reduce.16.cloned.1.call-done) | copy-start | bytes 196612
Sparse Core Ops, SparseCore 0:
  27.1 20.4 all-reduce.7
  62.8 104.6 all-reduce.9
  186.1 16.7 all-reduce.11
  216.0 104.6 all-reduce.13
  352.7 16.7 all-reduce.15
  382.7 104.6 all-reduce.17
where the time goes:
time: 501 us
  waiting for transfers between devices  369 us (74%)
  matrix products  95.5 us (19%)
  between operations  18.2 us (4%)
  blocking collectives  9.52 us (2%)
  other arithmetic  8.63 us (2%)
    psum x3, waiting for transfers between devices, collect(): return lax.psum(jnp.dot(terms, features, precision=HIGH), 'cells')  314 us
    dot_general x3, matrix products, row_sums(): lax.dot_general(coeffs, features, (((1,), (1,)), ((), ())), precision=HIG...  57.1 us
    psum x3, waiting for transfers between devices, row_sums(): summed = lax.psum(local_rows, 'feat')  54.3 us
    dot_general x3, matrix products, collect(): return lax.psum(jnp.dot(terms, features, precision=HIGH), 'cells')  38.3 us
  transfers between devices with their start and end apart: 6, of which 6 were waited for; matrix products, arithmetic and copies ran while one was open for 0% of the time, Pallas kernels for 0%

commit v1 on v0

v1 whole, which is shorter than its diff:
```python
import functools

import jax
import jax.numpy as jnp
from jax import lax
from jax.experimental import pallas as pl
from jax.experimental.pallas import tpu as pltpu
from jax.sharding import PartitionSpec as P

RIDGE = 0.01
MESH = pl.DeviceIdType.MESH
F32 = jnp.float32
BF16 = jnp.bfloat16


def split2(v):
    hi = v.astype(BF16)
    lo = (v - hi.astype(F32)).astype(BF16)
    return hi, lo


def stack2(v):
    hi = v.astype(BF16).astype(F32)
    return jnp.concatenate([hi, v - hi], axis=0).astype(BF16)


def total(v):
    return jnp.sum(jnp.sum(v, axis=1, keepdims=True), axis=0, keepdims=True)


def kernel(
    ncells, nfeat, count,
    x_hbm, lab_ref, w_ref, neww_ref, newl_ref,
    xs, xhi, xlo, part, logits, probs, image, t16, c16, gpart, rs, gbuf, qpart, rs2, qbuf,
    sc_f, sc_c,
    load_sem, fs_send, fs_recv, fsc_send, fsc_recv, rs_send, rs_recv, ag_send, ag_recv, cs_send, cs_recv,
):
    K, F = w_ref.shape
    NC, CH = xs.shape[0], xs.shape[1]
    W = rs.shape[2]
    owners = F // W
    TN = min(2 * W, F)
    per = TN // W
    tiles = F // TN
    KB = min(512, F)
    me = lax.axis_index("cells")
    mf = lax.axis_index("feat")

    loads = [pltpu.make_async_copy(x_hbm.at[pl.ds(i * CH, CH), :], xs.at[i], load_sem.at[i]) for i in range(NC)]
    for cp in loads:
        cp.start()
    barrier = pltpu.get_barrier_semaphore()
    for d in range(1, ncells):
        pl.semaphore_signal(barrier, inc=1, device_id={"cells": lax.rem(me + d, ncells)}, device_id_type=MESH)
    for d in range(1, nfeat):
        pl.semaphore_signal(barrier, inc=1, device_id={"feat": lax.rem(mf + d, nfeat)}, device_id_type=MESH)

    def feat_copy(ph, i, d, to):
        other = lax.rem(mf + d, nfeat)
        slot = mf if to else other
        return pltpu.make_async_remote_copy(
            src_ref=part.at[ph, i, mf], dst_ref=part.at[ph, i, slot],
            send_sem=fs_send.at[ph, i, other], recv_sem=fs_recv.at[ph, i, slot],
            device_id={"feat": other}, device_id_type=MESH)

    def feat_start(ph, i):
        for d in range(1, nfeat):
            feat_copy(ph, i, d, True).start()

    def feat_sum(ph, i):
        for d in range(1, nfeat):
            feat_copy(ph, i, d, False).wait_recv()
        out = part[ph, i, 0]
        for s in range(1, nfeat):
            out = out + part[ph, i, s]
        return out

    def fsc_copy(ph, d, to):
        other = lax.rem(mf + d, nfeat)
        slot = mf if to else other
        return pltpu.make_async_remote_copy(
            src_ref=sc_f.at[ph, mf], dst_ref=sc_f.at[ph, slot],
            send_sem=fsc_send.at[ph, other], recv_sem=fsc_recv.at[ph, slot],
            device_id={"feat": other}, device_id_type=MESH)

    def fsc_start(ph, a, b):
        rows = lax.broadcasted_iota(jnp.int32, (8, 128), 0)
        sc_f[ph, mf] = jnp.where(rows == 0, jnp.broadcast_to(a, (8, 128)), jnp.broadcast_to(b, (8, 128)))
        for d in range(1, nfeat):
            fsc_copy(ph, d, True).start()

    def fsc_sum(ph):
        for d in range(1, nfeat):
            fsc_copy(ph, d, False).wait_recv()
        out = sc_f[ph, 0]
        for s in range(1, nfeat):
            out = out + sc_f[ph, s]
        return out[0:1, 0:1], out[1:2, 0:1]

    def cs_copy(ph, d, to):
        other = lax.rem(me + d, ncells)
        slot = me if to else other
        return pltpu.make_async_remote_copy(
            src_ref=sc_c.at[ph, me], dst_ref=sc_c.at[ph, slot],
            send_sem=cs_send.at[ph, other], recv_sem=cs_recv.at[ph, slot],
            device_id={"cells": other}, device_id_type=MESH)

    def cs_start(ph, a):
        sc_c[ph, me] = jnp.broadcast_to(a, (8, 128))
        for d in range(1, ncells):
            cs_copy(ph, d, True).start()

    def cs_sum(ph):
        for d in range(1, ncells):
            cs_copy(ph, d, False).wait_recv()
        out = sc_c[ph, 0]
        for s in range(1, ncells):
            out = out + sc_c[ph, s]
        return out[0:1, 0:1]

    def rs_copy(ph, part_ref, buf, owner):
        return pltpu.make_async_remote_copy(
            src_ref=part_ref.at[:, pl.ds(pl.multiple_of(owner * W, W), W)], dst_ref=buf.at[me],
            send_sem=rs_send.at[ph, owner], recv_sem=rs_recv.at[ph, me],
            device_id={"cells": owner}, device_id_type=MESH)

    def rs_wait(ph, part_ref, buf, d):
        src = lax.rem(me + d, ncells)
        pltpu.make_async_remote_copy(
            src_ref=part_ref.at[:, pl.ds(0, W)], dst_ref=buf.at[src],
            send_sem=rs_send.at[ph, 0], recv_sem=rs_recv.at[ph, src],
            device_id={"cells": src}, device_id_type=MESH).wait_recv()

    def ag_copy(ph, buf, d):
        sl = buf.at[:, pl.ds(pl.multiple_of(me * W, W), W)]
        return pltpu.make_async_remote_copy(
            src_ref=sl, dst_ref=sl, send_sem=ag_send.at[ph, d], recv_sem=ag_recv.at[ph, me],
            device_id={"cells": lax.rem(me + d, ncells)}, device_id_type=MESH)

    def ag_wait(ph, buf, src):
        sl = buf.at[:, pl.ds(pl.multiple_of(src * W, W), W)]
        pltpu.make_async_remote_copy(
            src_ref=sl, dst_ref=sl, send_sem=ag_send.at[ph, 0], recv_sem=ag_recv.at[ph, src],
            device_id={"cells": src}, device_id_type=MESH).wait_recv()

    def collect(ph, part_ref, rsbuf, buf, add_ref, sign):
        first = lax.rem(me, owners) // per

        @pl.loop(0, tiles)
        def _(j):
            tile = lax.rem(first + j, tiles)
            cols = pl.ds(pl.multiple_of(tile * TN, TN), TN)
            t = t16[...]
            acc = jnp.dot(t, xhi[:, cols], preferred_element_type=F32)
            acc += jnp.dot(t, xlo[:, cols], preferred_element_type=F32)
            part_ref[:, cols] = acc[:K] + acc[K:]
            for u in range(per):
                owner = tile * per + u

                @pl.when(owner != me)
                def _():
                    rs_copy(ph, part_ref, rsbuf, owner).start()

        mine = pl.ds(pl.multiple_of(lax.rem(me, owners) * W, W), W)

        @pl.when(me < owners)
        def _():
            rsbuf[me] = part_ref[:, mine]
            for d in range(1, ncells):
                rs_wait(ph, part_ref, rsbuf, d)
            acc = rsbuf[0]
            for s in range(1, ncells):
                acc = acc + rsbuf[s]
            buf[:, mine] = sign * (acc / count) + RIDGE * add_ref[:, mine]
            for d in range(1, ncells):
                ag_copy(ph, buf, d).start()

        for s in range(owners):
            @pl.when(me != s)
            def _():
                ag_wait(ph, buf, s)

    def images(ph, i):
        rows = pl.ds(pl.multiple_of(i * CH, CH), CH)
        dims = (((1,), (1,)), ((), ()))
        c = c16[...]
        acc = lax.dot_general(c, xhi[rows, :], dims, preferred_element_type=F32)
        acc += lax.dot_general(c, xlo[rows, :], dims, preferred_element_type=F32)
        part[ph, i, mf] = acc[:K] + acc[K:]

    c16[...] = stack2(w_ref[...])
    for i in range(NC):
        loads[i].wait()

        @pl.loop(0, F // KB)
        def _(b):
            cols = pl.ds(pl.multiple_of(b * KB, KB), KB)
            hi, lo = split2(xs[i, :, cols])
            xhi[pl.ds(i * CH, CH), cols] = hi
            xlo[pl.ds(i * CH, CH), cols] = lo

        images(0, i)
        if i == 0:
            pl.semaphore_wait(barrier, ncells - 1 + nfeat - 1)
        feat_start(0, i)

    for i in range(NC):
        lg = feat_sum(0, i)
        e = jnp.exp(lg)
        p = e / jnp.sum(e, axis=0, keepdims=True)
        lab = lab_ref[:, pl.ds(i * CH, CH)]
        hot = (jnp.broadcast_to(lab, (K, CH)) == lax.broadcasted_iota(jnp.int32, (K, CH), 0)).astype(F32)
        logits[i] = lg
        probs[i] = p
        t16[:, pl.ds(i * CH, CH)] = stack2(p - hot)
    collect(0, gpart, rs, gbuf, w_ref, 1.0)

    g = gbuf[...]
    gbuf_neg = -g
    c16[...] = stack2(gbuf_neg)
    rr_part = total(g * g)
    fsc_start(0, rr_part, jnp.zeros_like(rr_part))

    @pl.loop(0, NC)
    def _(i):
        images(1, i)
        feat_start(1, i)

    s1 = jnp.zeros((1, 1), F32)
    for i in range(NC):
        im = feat_sum(1, i)
        p = probs[i]
        pim = p * im
        curv = pim - p * jnp.sum(pim, axis=0, keepdims=True)
        image[i] = im
        s1 = s1 + total(im * curv)
        t16[:, pl.ds(i * CH, CH)] = stack2(curv)
    cs_start(0, s1)
    rr, _ = fsc_sum(0)
    neww_ref[...] = -gbuf[...]
    collect(1, qpart, rs2, qbuf, neww_ref, 1.0)
    alpha = rr / (cs_sum(0) / count + RIDGE * rr)

    d1 = -gbuf[...]
    r1 = d1 - alpha * qbuf[...]
    c16[...] = stack2(r1)
    fsc_start(1, total(r1 * r1), total(r1 * d1))

    @pl.loop(0, NC)
    def _(i):
        images(2, i)
        feat_start(2, i)

    rr1, rd = fsc_sum(1)
    beta = rr1 / rr
    s2 = jnp.zeros((1, 1), F32)
    for i in range(NC):
        im1 = image[i]
        im = feat_sum(2, i) + beta * im1
        p = probs[i]
        pim = p * im
        curv = pim - p * jnp.sum(pim, axis=0, keepdims=True)
        s2 = s2 + total(im * curv)
        logits[i] = logits[i] + alpha * im1
        image[i] = im
    cs_start(1, s2)
    dd2 = rr1 + 2.0 * beta * rd + beta * beta * rr
    d1 = -gbuf[...]
    d2 = d1 - alpha * qbuf[...] + beta * d1
    first = w_ref[...] + alpha * d1
    alpha2 = rr1 / (cs_sum(1) / count + RIDGE * dd2)
    neww_ref[...] = first + alpha2 * d2
    for i in range(NC):
        newl_ref[:, pl.ds(i * CH, CH)] = logits[i] + alpha2 * image[i]

    for ph in range(3):
        for i in range(NC):
            for d in range(1, nfeat):
                feat_copy(ph, i, d, True).wait_send()
    for ph in range(2):
        for d in range(1, nfeat):
            fsc_copy(ph, d, True).wait_send()
        for d in range(1, ncells):
            cs_copy(ph, d, True).wait_send()
        pr, rb, bb = ((gpart, rs, gbuf), (qpart, rs2, qbuf))[ph]
        for s in range(owners):
            @pl.when(me != s)
            def _():
                rs_copy(ph, pr, rb, s).wait_send()

        @pl.when(me < owners)
        def _():
            for d in range(1, ncells):
                ag_copy(ph, bb, d).wait_send()


def on_device(ncells, nfeat, features, labels, weights):
    rows, F = features.shape
    K = weights.shape[0]
    NC = 8 if rows % 1024 == 0 else 1
    CH = rows // NC
    W = max(128, F // ncells)
    count = rows * ncells * 1.0
    vm = pltpu.VMEM
    dma = pltpu.SemaphoreType.DMA
    vmem = pl.BlockSpec(memory_space=pltpu.VMEM)
    return pl.pallas_call(
        functools.partial(kernel, ncells, nfeat, count),
        out_shape=(jax.ShapeDtypeStruct((K, F), F32), jax.ShapeDtypeStruct((K, rows), F32)),
        in_specs=[pl.BlockSpec(memory_space=pl.ANY), vmem, vmem],
        out_specs=(vmem, vmem),
        scratch_shapes=[
            vm((NC, CH, F), F32), vm((rows, F), BF16), vm((rows, F), BF16),
            vm((3, NC, nfeat, K, CH), F32), vm((NC, K, CH), F32), vm((NC, K, CH), F32), vm((NC, K, CH), F32),
            vm((2 * K, rows), BF16), vm((2 * K, F), BF16),
            vm((K, F), F32), vm((ncells, K, W), F32), vm((K, F), F32),
            vm((K, F), F32), vm((ncells, K, W), F32), vm((K, F), F32),
            vm((2, nfeat, 8, 128), F32), vm((2, ncells, 8, 128), F32),
            dma((NC,)), dma((3, NC, nfeat)), dma((3, NC, nfeat)), dma((2, nfeat)), dma((2, nfeat)),
            dma((2, ncells)), dma((2, ncells)), dma((2, ncells)), dma((2, ncells)), dma((2, ncells)), dma((2, ncells)),
        ],
        compiler_params=pltpu.CompilerParams(
            collective_id=0, has_side_effects=True, vmem_limit_bytes=56 * 1024 * 1024),
    )(features, labels[None, :], weights)


def solution(mesh):
    return jax.shard_map(
        functools.partial(on_device, mesh.shape["cells"], mesh.shape["feat"]),
        mesh=mesh,
        in_specs=(P("cells", "feat"), P("cells"), P(None, "feat")),
        out_specs=(P(None, "feat"), P(None, "cells")),
        check_vma=False,
    )
```

time: 501 us -> 66.2 us (0.13)
  waiting for transfers between devices: 369 us -> 0 us
  matrix products: 95.5 us -> 0 us
  Pallas kernels: 0 us -> 62.3 us
  between operations: 18.2 us -> 0.64 us
  blocking collectives: 9.52 us -> 0 us
  other arithmetic: 8.63 us -> 0 us
    psum x6 -> x0, waiting for transfers between devices: 368 us -> none  [the longest x3 314 us: collect(): return lax.psum(jnp.dot(terms, features, precision=HIGH), 'cells')]
    dot_general x6 -> x0, matrix products: 95.5 us -> none  [the longest x3 57.1 us: row_sums(): lax.dot_general(coeffs, features, (((1,), (1,)), ((), ())), precision=HIG...]
    pallas_call x0 -> x1, Pallas kernels: none -> 62.3 us  [on_device(): pl.pallas_call(functools.partial(kernel, ncells, nfeat, count), out_shape...]
    psum x3 -> x0, blocking collectives: 9.52 us -> none  [total(): return lax.psum(packed, 'feat')]
    reduce_sum x6 -> x0, other arithmetic: 7.1 us -> none  [the longest x3 4.41 us: inner(): return total(jnp.sum(left * right))]
  transfers between devices with their start and end apart: 6 -> 0, of which waited for: 6 -> 0; matrix products, arithmetic and copies ran while one was open for 0% -> 0% of each run, Pallas kernels for 0% -> 0%
where the time goes in v1:
time: 66.2 us; the launch traced here: 65.9 us
  Pallas kernels  62.3 us (94%)
  local copies, waits for them, and re-layouts  2.95 us (4%)
    pallas_call x1, Pallas kernels, on_device(): pl.pallas_call(functools.partial(kernel, ncells, nfeat, count), out_shape...  62.3 us
    unnamed x2, local copies, waits for them, and re-layouts  2.95 us

profile of v1, /device:TPU:0, one launch (start us, length us, event | category | flops | bytes accessed | tf_op | source)
XLA Modules:
  0.0 65.9 jit_solution(8285015315386147000)
XLA Ops:
  0.6 62.3 %shard_map.50 = (f32[8,2048]{1,0:T(8,128)}, f32[8,2048]{1,0:T(8,128)}) custom-call(f32[2048,2048]{1,0:T(8,128)} %x_hbm.1, s32[1,2048]{1,0:T(1,128)} %bitcast.1, f32[8,2048]{1,0:T(8,128)} %w_ref.1), custom_call_target="tpu_custom_call" | custom-call | tf_op jit(solution)/shard_map/pallas_call | solution.py:307
  63.0 1.5 %copy.7 = f32[8,2048]{1,0:T(8,128)} copy(f32[8,2048]{1,0:T(8,128)} %get-tuple-element.4) | data formatting | bytes 131072
  64.5 1.5 %copy.8 = f32[8,2048]{1,0:T(8,128)} copy(f32[8,2048]{1,0:T(8,128)} %get-tuple-element.5) | data formatting | bytes 131072

commit v2 on v1

--- a/solution.py
+++ b/solution.py
@@ -31,7 +31,7 @@
 def kernel(
     ncells, nfeat, count,
     x_hbm, lab_ref, w_ref, neww_ref, newl_ref,
-    xs, xhi, xlo, part, logits, probs, image, t16, c16, gpart, rs, gbuf, qpart, rs2, qbuf,
+    xs, xhi, xlo, thi, tlo, part, logits, probs, image, t16, c16, gpart, rs, gbuf, qpart, rs2, qbuf,
     sc_f, sc_c,
     load_sem, fs_send, fs_recv, fsc_send, fsc_recv, rs_send, rs_recv, ag_send, ag_recv, cs_send, cs_recv,
 ):
@@ -39,21 +39,32 @@
     NC, CH = xs.shape[0], xs.shape[1]
     W = rs.shape[2]
     owners = F // W
-    TN = min(2 * W, F)
+    TN = min(4 * W, F)
     per = TN // W
     tiles = F // TN
-    KB = min(512, F)
+    KB = min(256, F)
     me = lax.axis_index("cells")
     mf = lax.axis_index("feat")
+
+    def ranked(j, own, n):
+        above, below = n - 1 - own, own
+        up = jnp.where(j < above, n - 1 - j, j - above)
+        down = jnp.where(j < below, j, n - 1 - (j - below))
+        return jnp.where(2 * own < n, up, down)
 
     loads = [pltpu.make_async_copy(x_hbm.at[pl.ds(i * CH, CH), :], xs.at[i], load_sem.at[i]) for i in range(NC)]
     for cp in loads:
         cp.start()
     barrier = pltpu.get_barrier_semaphore()
     for d in range(1, ncells):
-        pl.semaphore_signal(barrier, inc=1, device_id={"cells": lax.rem(me + d, ncells)}, device_id_type=MESH)
+        pl.semaphore_signal(barrier, inc=1, device_id={"cells": ranked(d - 1, me, ncells)}, device_id_type=MESH)
     for d in range(1, nfeat):
         pl.semaphore_signal(barrier, inc=1, device_id={"feat": lax.rem(mf + d, nfeat)}, device_id_type=MESH)
+
+    mid = lax.rem(me, owners) // per
+
+    def far_first(j):
+        return ranked(j, mid, tiles)
 
     def feat_copy(ph, i, d, to):
         other = lax.rem(mf + d, nfeat)
@@ -98,7 +109,7 @@
         return out[0:1, 0:1], out[1:2, 0:1]
 
     def cs_copy(ph, d, to):
-        other = lax.rem(me + d, ncells)
+        other = ranked(d - 1, me, ncells)
         slot = me if to else other
         return pltpu.make_async_remote_copy(
             src_ref=sc_c.at[ph, me], dst_ref=sc_c.at[ph, slot],
@@ -135,7 +146,7 @@
         sl = buf.at[:, pl.ds(pl.multiple_of(me * W, W), W)]
         return pltpu.make_async_remote_copy(
             src_ref=sl, dst_ref=sl, send_sem=ag_send.at[ph, d], recv_sem=ag_recv.at[ph, me],
-            device_id={"cells": lax.rem(me + d, ncells)}, device_id_type=MESH)
+            device_id={"cells": ranked(d - 1, me, ncells)}, device_id_type=MESH)
 
     def ag_wait(ph, buf, src):
         sl = buf.at[:, pl.ds(pl.multiple_of(src * W, W), W)]
@@ -144,11 +155,9 @@
             device_id={"cells": src}, device_id_type=MESH).wait_recv()
 
     def collect(ph, part_ref, rsbuf, buf, add_ref, sign):
-        first = lax.rem(me, owners) // per
-
         @pl.loop(0, tiles)
         def _(j):
-            tile = lax.rem(first + j, tiles)
+            tile = far_first(j)
             cols = pl.ds(pl.multiple_of(tile * TN, TN), TN)
             t = t16[...]
             acc = jnp.dot(t, xhi[:, cols], preferred_element_type=F32)
@@ -175,34 +184,67 @@
             for d in range(1, ncells):
                 ag_copy(ph, buf, d).start()
 
-        for s in range(owners):
-            @pl.when(me != s)
-            def _():
-                ag_wait(ph, buf, s)
-
-    def images(ph, i):
+    def image_pass(ph, buf, coeffs):
+        def one(j, last):
+            tile = far_first(tiles - 1 - j)
+            for u in range(per):
+                owner = tile * per + u
+
+                @pl.when(owner != me)
+                def _():
+                    ag_wait(ph - 1, buf, owner)
+            cols = pl.ds(pl.multiple_of(tile * TN, TN), TN)
+            c = stack2(coeffs(cols))
+            for i in range(NC):
+                acc = jnp.dot(c, thi[cols, pl.ds(i * CH, CH)], preferred_element_type=F32)
+                acc += jnp.dot(c, tlo[cols, pl.ds(i * CH, CH)], preferred_element_type=F32)
+                part[ph, i, mf] = part[ph, i, mf] + (acc[:K] + acc[K:])
+                if last:
+                    feat_start(ph, i)
+
+        for i in range(NC):
+            part[ph, i, mf] = jnp.zeros((K, CH), F32)
+        if tiles > 1:
+            @pl.loop(0, tiles - 1)
+            def _(j):
+                one(j, False)
+        one(tiles - 1, True)
+
+    c16[...] = stack2(w_ref[...])
+    steps = F // KB
+    unroll = 8 if steps % 8 == 0 else 1
+
+    @pl.loop(0, NC)
+    def _(i):
+        pltpu.make_async_copy(x_hbm.at[pl.ds(0, CH), :], xs.at[i], load_sem.at[i]).wait()
         rows = pl.ds(pl.multiple_of(i * CH, CH), CH)
-        dims = (((1,), (1,)), ((), ()))
-        c = c16[...]
-        acc = lax.dot_general(c, xhi[rows, :], dims, preferred_element_type=F32)
-        acc += lax.dot_general(c, xlo[rows, :], dims, preferred_element_type=F32)
-        part[ph, i, mf] = acc[:K] + acc[K:]
-
-    c16[...] = stack2(w_ref[...])
-    for i in range(NC):
-        loads[i].wait()
-
-        @pl.loop(0, F // KB)
+        part[0, i, mf] = jnp.zeros((K, CH), F32)
+
+        @pl.loop(0, steps // unroll)
         def _(b):
-            cols = pl.ds(pl.multiple_of(b * KB, KB), KB)
-            hi, lo = split2(xs[i, :, cols])
-            xhi[pl.ds(i * CH, CH), cols] = hi
-            xlo[pl.ds(i * CH, CH), cols] = lo
-
-        images(0, i)
-        if i == 0:
+            acc = jnp.zeros((2 * K, CH), F32)
+            for v in range(unroll):
+                cols = pl.ds(pl.multiple_of((b * unroll + v) * KB, KB), KB)
+                hi, lo = split2(xs[i, :, cols])
+                xhi[rows, cols] = hi
+                xlo[rows, cols] = lo
+                hit, lot = hi.T, lo.T
+                thi[cols, rows] = hit
+                tlo[cols, rows] = lot
+                c = c16[:, cols]
+                acc += jnp.dot(c, hit, preferred_element_type=F32)
+                acc += jnp.dot(c, lot, preferred_element_type=F32)
+            part[0, i, mf] = part[0, i, mf] + (acc[:K] + acc[K:])
+
+        @pl.when(i == NC - 2)
+        def _():
             pl.semaphore_wait(barrier, ncells - 1 + nfeat - 1)
-        feat_start(0, i)
+            for k in range(NC - 2):
+                feat_start(0, k)
+
+        @pl.when(i >= NC - 2)
+        def _():
+            feat_start(0, i)
 
     for i in range(NC):
         lg = feat_sum(0, i)
@@ -215,16 +257,11 @@
         t16[:, pl.ds(i * CH, CH)] = stack2(p - hot)
     collect(0, gpart, rs, gbuf, w_ref, 1.0)
 
+    image_pass(1, gbuf, lambda cols: -gbuf[:, cols])
     g = gbuf[...]
-    gbuf_neg = -g
-    c16[...] = stack2(gbuf_neg)
     rr_part = total(g * g)
     fsc_start(0, rr_part, jnp.zeros_like(rr_part))
-
-    @pl.loop(0, NC)
-    def _(i):
-        images(1, i)
-        feat_start(1, i)
+    neww_ref[...] = -g
 
     s1 = jnp.zeros((1, 1), F32)
     for i in range(NC):
@@ -237,19 +274,13 @@
         t16[:, pl.ds(i * CH, CH)] = stack2(curv)
     cs_start(0, s1)
     rr, _ = fsc_sum(0)
-    neww_ref[...] = -gbuf[...]
     collect(1, qpart, rs2, qbuf, neww_ref, 1.0)
     alpha = rr / (cs_sum(0) / count + RIDGE * rr)
 
+    image_pass(2, qbuf, lambda cols: -gbuf[:, cols] - alpha * qbuf[:, cols])
     d1 = -gbuf[...]
     r1 = d1 - alpha * qbuf[...]
-    c16[...] = stack2(r1)
     fsc_start(1, total(r1 * r1), total(r1 * d1))
-
-    @pl.loop(0, NC)
-    def _(i):
-        images(2, i)
-        feat_start(2, i)
 
     rr1, rd = fsc_sum(1)
     beta = rr1 / rr
@@ -297,7 +328,7 @@
 def on_device(ncells, nfeat, features, labels, weights):
     rows, F = features.shape
     K = weights.shape[0]
-    NC = 8 if rows % 1024 == 0 else 1
+    NC = 4 if rows % 512 == 0 else 2
     CH = rows // NC
     W = max(128, F // ncells)
     count = rows * ncells * 1.0
@@ -310,7 +341,7 @@
         in_specs=[pl.BlockSpec(memory_space=pl.ANY), vmem, vmem],
         out_specs=(vmem, vmem),
         scratch_shapes=[
-            vm((NC, CH, F), F32), vm((rows, F), BF16), vm((rows, F), BF16),
+            vm((NC, CH, F), F32), vm((rows, F), BF16), vm((rows, F), BF16), vm((F, rows), BF16), vm((F, rows), BF16),
             vm((3, NC, nfeat, K, CH), F32), vm((NC, K, CH), F32), vm((NC, K, CH), F32), vm((NC, K, CH), F32),
             vm((2 * K, rows), BF16), vm((2 * K, F), BF16),
             vm((K, F), F32), vm((ncells, K, W), F32), vm((K, F), F32),

time: 66.2 us -> 51.1 us (0.77)
  Pallas kernels: 62.3 us -> 47.2 us
    pallas_call x1, Pallas kernels: 62.3 us -> 47.2 us  [on_device(): pl.pallas_call(functools.partial(kernel, ncells, nfeat, count), out_shape...]
where the time goes in v2:
time: 51.1 us; the launch traced here: 50.8 us
  Pallas kernels  47.2 us (92%)
  local copies, waits for them, and re-layouts  2.95 us (6%)
  between operations  0.64 us (1%)
    pallas_call x1, Pallas kernels, on_device(): pl.pallas_call(functools.partial(kernel, ncells, nfeat, count), out_shape...  47.2 us
    unnamed x2, local copies, waits for them, and re-layouts  2.95 us

profile of v2, /device:TPU:0, one launch (start us, length us, event | category | flops | bytes accessed | tf_op | source)
XLA Modules:
  0.0 50.8 jit_solution(15573127982464001200)
XLA Ops:
  0.6 47.2 %shard_map.50 = (f32[8,2048]{1,0:T(8,128)}, f32[8,2048]{1,0:T(8,128)}) custom-call(f32[2048,2048]{1,0:T(8,128)} %x_hbm.1, s32[1,2048]{1,0:T(1,128)} %bitcast.1, f32[8,2048]{1,0:T(8,128)} %w_ref.1), custom_call_target="tpu_custom_call" | custom-call | tf_op jit(solution)/shard_map/pallas_call | solution.py:338
  47.9 1.5 %copy.7 = f32[8,2048]{1,0:T(8,128)} copy(f32[8,2048]{1,0:T(8,128)} %get-tuple-element.4) | data formatting | bytes 131072
  49.4 1.5 %copy.8 = f32[8,2048]{1,0:T(8,128)} copy(f32[8,2048]{1,0:T(8,128)} %get-tuple-element.5) | data formatting | bytes 131072
